TPU v7x, 512 devices: a whole 4x8x8 slice. The times are simulated.
512 devices in a mesh: node: 16 (over z, core), dev: 32 (over y, x).
Axes of the slice: x: 4, y: 8, z: 8, core: 2. Of those that a mesh axis runs over, the one named last changes fastest.
Arguments:
- amps: float32 [16, 32, 32, 1024], P('node', 'dev'), may hold values from -6 to 6
- amp_tile: int32 [16, 32], replicated, may hold values from 0 to 31, each once within a row
- ints: float32 [16, 32, 1024, 1024], P('node', 'dev'), may hold values from -0.1875 to 0.1875
- tasks: int32 [16, 256, 2], replicated, may hold values from 0 to 31, as said below
- pair_energy: float32 [16, 32], P('node', 'dev'), may hold values from -3 to -1
- virt_energy: float32 [16, 1024], replicated, may hold values from 0.5 to 3
Outputs:
- resid: float32 [16, 32, 16384], P('node', 'dev')
Inputs may be any that keep to these rules, and one draw needn't show every extreme that they name: Each row amp_tile[n] is a permutation of the 32 contracted tile pairs. `tasks`: the first column names an output tile pair below 16, the second a contracted tile pair below 32; the (ab, cd) pairs of one pair block are distinct.
All inputs are finite; a program needn't handle non-finite values.
Results may differ from a plain program's by a relative error of at most 0.0003.
Values sent between devices are 32-bit elements; how exact they have to be, the bound alone decides.
A program may use at most 64 MiB of HBM per device.

v0:
```python
import jax
import jax.numpy as jnp
from jax import lax
from jax.sharding import PartitionSpec as P


def tile_product(left, right):
    return lax.dot_general(
        left,
        right,
        (((1,), (1,)), ((), ())),
        precision=lax.Precision.HIGHEST,
        preferred_element_type=jnp.float32,
    )


def on_device(amps, amp_tile, ints, tasks, pair_energy, virt_energy):
    my_dev = lax.axis_index("dev")
    my_node = lax.axis_index("node")
    pairs = amps.shape[2]
    width = amps.shape[3]
    block_count = amp_tile.shape[0]
    my_slots = lax.dynamic_index_in_dim(amp_tile, my_node, 0, keepdims=False)
    wanted = my_slots == my_dev
    my_amp = jnp.sum(
        jnp.where(wanted[:, None, None], lax.all_gather(amps, "dev", axis=1, tiled=True)[0], 0.0),
        axis=0,
    )
    hit_mask = (tasks[:, :, 0] == my_node) & (tasks[:, :, 1] == my_dev)
    hits = jnp.sum(hit_mask.astype(jnp.int32), axis=1)
    my_tile = ints[0, 0]
    piece = lax.all_gather(my_amp[None], "node", axis=0, tiled=True)

    def one_block(position, acc):
        amp_block = lax.dynamic_index_in_dim(piece, position, 0, keepdims=False)

        def add_term(inner):
            current = lax.dynamic_slice(inner, (position, 0, 0), (1, pairs, width))
            update = current + tile_product(amp_block, my_tile)[None]
            return lax.dynamic_update_slice(inner, update, (position, 0, 0))

        return lax.cond(hits[position] > 0, add_term, lambda inner: inner, acc)

    partial_ladder = lax.fori_loop(
        0, piece.shape[0], one_block, jnp.zeros((block_count, pairs, width), jnp.float32)
    )
    moved = lax.all_to_all(partial_ladder, "node", split_axis=0, concat_axis=2, tiled=True)
    ladder = lax.psum_scatter(moved, "dev", scatter_dimension=1, tiled=True)
    denominator = pair_energy[:, :, None] - virt_energy.reshape(1, 1, -1)
    return ladder / denominator


def solution(mesh):
    in_specs = (
        P("node", "dev", None, None),
        P(),
        P("node", "dev", None, None),
        P(),
        P("node", "dev"),
        P(),
    )
    out_specs = P("node", "dev", None)
    return jax.shard_map(
        on_device, mesh=mesh, in_specs=in_specs, out_specs=out_specs, check_vma=False
    )
```

profile of v0, /device:TPU:1, one launch (start us, length us, event | category | flops | bytes accessed | tf_op | source)
XLA Modules:
  0.0 467.4 jit_solution(10859346802606807565)
XLA Ops:
  6.5 0.0 all-gather.4.cloned.1.call-start
  6.5 0.7 all-gather.4.cloned.1.call-update
  7.3 0.0 all-gather.6.cloned.1.call-start
  7.3 0.7 compare_bitcast_fusion
  8.0 0.0 copy-start.1
  8.0 92.5 %all-gather.4.cloned.1.call-done = f32[1,32,32,1024]{3,2,0,1:T(8,128)} async-done(((f32[1,1,32,1024]{3,2,0,1:T(8,128)}), f32[1,32,32,1024]{3,2,0,1:T(8,128)}) %all-gather.4.cloned.1.call-update) | async-done | bytes 4194320 | tf_op jit(solution)/shard_map/all_gather | solution.py:26
  100.5 3.3 fusion.5
  103.8 0.0 all-gather.6.cloned.1.call-update
  103.9 0.0 all-reduce.3.cloned.1.call-start
  103.9 0.0 copy-done.1
  103.9 0.4 fusion.6
  104.3 43.5 %all-gather.6.cloned.1.call-done = f32[512,1024]{1,0:T(8,128)} async-done(((f32[32,1024]{1,0:T(8,128)}), f32[512,1024]{1,0:T(8,128)}) %all-gather.6.cloned.1.call-update) | async-done | bytes 2097168 | tf_op jit(solution)/shard_map/all_gather | solution.py:32
  147.8 0.2 broadcast_in_dim.24
  148.0 74.0 %while.16 = (s32[]{:T(128)}, f32[16,32,1024]{2,1,0:T(8,128)S(1)}, s32[16]{0:T(128)S(1)}, f32[16,32,1024]{2,1,0:T(8,128)}, f32[1024,1024]{1,0:T(8,128)}, /*index=5*/s32[]{:T(128)}, s32[1]{0:T(128)}) while((s32[]{:T(128)}, f32[16,32,1024]{2,1,0:T(8,128)S(1)}, s32[16]{0:T(128)S(1)}, f32[16,32,1024]{2,1,0:T(8,128)}, f32[1024,1024]{1,0:T(8,128)}, ...), condition=%wide.region_5.6_spmd, body=%wide.region_2.5_spmd.sunk | while | flops 402685952 | bytes 4588213 | solution.py:44
  148.1 0.6 dynamic_slice.34
  149.2 6.1 %conditional.2 = (f32[16,32,1024]{2,1,0:T(8,128)S(1)}) conditional(s32[]{:T(128)} %bitcast.30, f32[16,32,1024]{2,1,0:T(8,128)S(1)} %get-tuple-element.183, (s32[]{:T(128)}, f32[16,32,1024]{2,1,0:T(8,128)S(1)}, f32[16,32,1024]{2,1,0:T(8,128)}, f32[1024,1024]{1,0:T(8,128)}) %tuple.41), branch_computations={%region_3.3_spmd, %region_4.4_spmd} | conditional | flops 402685952 | bytes 4588078 | solution.py:42
  149.2 6.1 %fusion.1 = f32[16,32,1024]{2,1,0:T(8,128)S(1)} fusion(f32[16,32,1024]{2,1,0:T(8,128)S(1)} %get-tuple-element.122, s32[]{:T(128)S(6)} %select_n.17, f32[1024,1024]{1,0:T(8,128)} %get-tuple-element.125, f32[16,32,1024]{2,1,0:T(8,128)} %get-tuple-element.124, s32[]{:T(128)} %get-tuple-element.123), kind=kOutput, calls=%fused_computation.2 | convolution fusion | flops 402685952 | bytes 4588036 | tf_op jit(solution)/shard_map/while/body/eval_jaxpr/cond/branch_1_fun/dot_general | solution.py:8
  155.4 0.6 dynamic_slice.34
  156.5 6.1 %conditional.2 = (f32[16,32,1024]{2,1,0:T(8,128)S(1)}) conditional(s32[]{:T(128)} %bitcast.30, f32[16,32,1024]{2,1,0:T(8,128)S(1)} %get-tuple-element.183, (s32[]{:T(128)}, f32[16,32,1024]{2,1,0:T(8,128)S(1)}, f32[16,32,1024]{2,1,0:T(8,128)}, f32[1024,1024]{1,0:T(8,128)}) %tuple.41), branch_computations={%region_3.3_spmd, %region_4.4_spmd} | conditional | flops 402685952 | bytes 4588078 | solution.py:42
  156.5 6.1 %fusion.1 = f32[16,32,1024]{2,1,0:T(8,128)S(1)} fusion(f32[16,32,1024]{2,1,0:T(8,128)S(1)} %get-tuple-element.122, s32[]{:T(128)S(6)} %select_n.17, f32[1024,1024]{1,0:T(8,128)} %get-tuple-element.125, f32[16,32,1024]{2,1,0:T(8,128)} %get-tuple-element.124, s32[]{:T(128)} %get-tuple-element.123), kind=kOutput, calls=%fused_computation.2 | convolution fusion | flops 402685952 | bytes 4588036 | tf_op jit(solution)/shard_map/while/body/eval_jaxpr/cond/branch_1_fun/dot_general | solution.py:8
  162.7 0.6 dynamic_slice.34
  163.8 6.1 %conditional.2 = (f32[16,32,1024]{2,1,0:T(8,128)S(1)}) conditional(s32[]{:T(128)} %bitcast.30, f32[16,32,1024]{2,1,0:T(8,128)S(1)} %get-tuple-element.183, (s32[]{:T(128)}, f32[16,32,1024]{2,1,0:T(8,128)S(1)}, f32[16,32,1024]{2,1,0:T(8,128)}, f32[1024,1024]{1,0:T(8,128)}) %tuple.41), branch_computations={%region_3.3_spmd, %region_4.4_spmd} | conditional | flops 402685952 | bytes 4588078 | solution.py:42
  163.8 6.1 %fusion.1 = f32[16,32,1024]{2,1,0:T(8,128)S(1)} fusion(f32[16,32,1024]{2,1,0:T(8,128)S(1)} %get-tuple-element.122, s32[]{:T(128)S(6)} %select_n.17, f32[1024,1024]{1,0:T(8,128)} %get-tuple-element.125, f32[16,32,1024]{2,1,0:T(8,128)} %get-tuple-element.124, s32[]{:T(128)} %get-tuple-element.123), kind=kOutput, calls=%fused_computation.2 | convolution fusion | flops 402685952 | bytes 4588036 | tf_op jit(solution)/shard_map/while/body/eval_jaxpr/cond/branch_1_fun/dot_general | solution.py:8
  170.0 0.6 dynamic_slice.34
  171.1 0.6 dynamic_slice.34
  172.3 6.1 %conditional.2 = (f32[16,32,1024]{2,1,0:T(8,128)S(1)}) conditional(s32[]{:T(128)} %bitcast.30, f32[16,32,1024]{2,1,0:T(8,128)S(1)} %get-tuple-element.183, (s32[]{:T(128)}, f32[16,32,1024]{2,1,0:T(8,128)S(1)}, f32[16,32,1024]{2,1,0:T(8,128)}, f32[1024,1024]{1,0:T(8,128)}) %tuple.41), branch_computations={%region_3.3_spmd, %region_4.4_spmd} | conditional | flops 402685952 | bytes 4588078 | solution.py:42
  172.3 6.1 %fusion.1 = f32[16,32,1024]{2,1,0:T(8,128)S(1)} fusion(f32[16,32,1024]{2,1,0:T(8,128)S(1)} %get-tuple-element.122, s32[]{:T(128)S(6)} %select_n.17, f32[1024,1024]{1,0:T(8,128)} %get-tuple-element.125, f32[16,32,1024]{2,1,0:T(8,128)} %get-tuple-element.124, s32[]{:T(128)} %get-tuple-element.123), kind=kOutput, calls=%fused_computation.2 | convolution fusion | flops 402685952 | bytes 4588036 | tf_op jit(solution)/shard_map/while/body/eval_jaxpr/cond/branch_1_fun/dot_general | solution.py:8
  178.4 0.6 dynamic_slice.34
  179.6 6.1 %conditional.2 = (f32[16,32,1024]{2,1,0:T(8,128)S(1)}) conditional(s32[]{:T(128)} %bitcast.30, f32[16,32,1024]{2,1,0:T(8,128)S(1)} %get-tuple-element.183, (s32[]{:T(128)}, f32[16,32,1024]{2,1,0:T(8,128)S(1)}, f32[16,32,1024]{2,1,0:T(8,128)}, f32[1024,1024]{1,0:T(8,128)}) %tuple.41), branch_computations={%region_3.3_spmd, %region_4.4_spmd} | conditional | flops 402685952 | bytes 4588078 | solution.py:42
  179.6 6.1 %fusion.1 = f32[16,32,1024]{2,1,0:T(8,128)S(1)} fusion(f32[16,32,1024]{2,1,0:T(8,128)S(1)} %get-tuple-element.122, s32[]{:T(128)S(6)} %select_n.17, f32[1024,1024]{1,0:T(8,128)} %get-tuple-element.125, f32[16,32,1024]{2,1,0:T(8,128)} %get-tuple-element.124, s32[]{:T(128)} %get-tuple-element.123), kind=kOutput, calls=%fused_computation.2 | convolution fusion | flops 402685952 | bytes 4588036 | tf_op jit(solution)/shard_map/while/body/eval_jaxpr/cond/branch_1_fun/dot_general | solution.py:8
  185.8 0.6 dynamic_slice.34
  186.9 6.1 %conditional.2 = (f32[16,32,1024]{2,1,0:T(8,128)S(1)}) conditional(s32[]{:T(128)} %bitcast.30, f32[16,32,1024]{2,1,0:T(8,128)S(1)} %get-tuple-element.183, (s32[]{:T(128)}, f32[16,32,1024]{2,1,0:T(8,128)S(1)}, f32[16,32,1024]{2,1,0:T(8,128)}, f32[1024,1024]{1,0:T(8,128)}) %tuple.41), branch_computations={%region_3.3_spmd, %region_4.4_spmd} | conditional | flops 402685952 | bytes 4588078 | solution.py:42
  186.9 6.1 %fusion.1 = f32[16,32,1024]{2,1,0:T(8,128)S(1)} fusion(f32[16,32,1024]{2,1,0:T(8,128)S(1)} %get-tuple-element.122, s32[]{:T(128)S(6)} %select_n.17, f32[1024,1024]{1,0:T(8,128)} %get-tuple-element.125, f32[16,32,1024]{2,1,0:T(8,128)} %get-tuple-element.124, s32[]{:T(128)} %get-tuple-element.123), kind=kOutput, calls=%fused_computation.2 | convolution fusion | flops 402685952 | bytes 4588036 | tf_op jit(solution)/shard_map/while/body/eval_jaxpr/cond/branch_1_fun/dot_general | solution.py:8
  193.1 0.6 dynamic_slice.34
  194.2 0.6 dynamic_slice.34
  195.4 6.1 %conditional.2 = (f32[16,32,1024]{2,1,0:T(8,128)S(1)}) conditional(s32[]{:T(128)} %bitcast.30, f32[16,32,1024]{2,1,0:T(8,128)S(1)} %get-tuple-element.183, (s32[]{:T(128)}, f32[16,32,1024]{2,1,0:T(8,128)S(1)}, f32[16,32,1024]{2,1,0:T(8,128)}, f32[1024,1024]{1,0:T(8,128)}) %tuple.41), branch_computations={%region_3.3_spmd, %region_4.4_spmd} | conditional | flops 402685952 | bytes 4588078 | solution.py:42
  195.4 6.1 %fusion.1 = f32[16,32,1024]{2,1,0:T(8,128)S(1)} fusion(f32[16,32,1024]{2,1,0:T(8,128)S(1)} %get-tuple-element.122, s32[]{:T(128)S(6)} %select_n.17, f32[1024,1024]{1,0:T(8,128)} %get-tuple-element.125, f32[16,32,1024]{2,1,0:T(8,128)} %get-tuple-element.124, s32[]{:T(128)} %get-tuple-element.123), kind=kOutput, calls=%fused_computation.2 | convolution fusion | flops 402685952 | bytes 4588036 | tf_op jit(solution)/shard_map/while/body/eval_jaxpr/cond/branch_1_fun/dot_general | solution.py:8
  201.5 0.6 dynamic_slice.34
  202.7 0.6 dynamic_slice.34
  203.9 6.1 %conditional.2 = (f32[16,32,1024]{2,1,0:T(8,128)S(1)}) conditional(s32[]{:T(128)} %bitcast.30, f32[16,32,1024]{2,1,0:T(8,128)S(1)} %get-tuple-element.183, (s32[]{:T(128)}, f32[16,32,1024]{2,1,0:T(8,128)S(1)}, f32[16,32,1024]{2,1,0:T(8,128)}, f32[1024,1024]{1,0:T(8,128)}) %tuple.41), branch_computations={%region_3.3_spmd, %region_4.4_spmd} | conditional | flops 402685952 | bytes 4588078 | solution.py:42
  203.9 6.1 %fusion.1 = f32[16,32,1024]{2,1,0:T(8,128)S(1)} fusion(f32[16,32,1024]{2,1,0:T(8,128)S(1)} %get-tuple-element.122, s32[]{:T(128)S(6)} %select_n.17, f32[1024,1024]{1,0:T(8,128)} %get-tuple-element.125, f32[16,32,1024]{2,1,0:T(8,128)} %get-tuple-element.124, s32[]{:T(128)} %get-tuple-element.123), kind=kOutput, calls=%fused_computation.2 | convolution fusion | flops 402685952 | bytes 4588036 | tf_op jit(solution)/shard_map/while/body/eval_jaxpr/cond/branch_1_fun/dot_general | solution.py:8
  210.0 0.6 dynamic_slice.34
  211.2 0.6 dynamic_slice.34
  212.4 0.6 dynamic_slice.34
  213.6 0.6 dynamic_slice.34
  214.7 6.1 %conditional.2 = (f32[16,32,1024]{2,1,0:T(8,128)S(1)}) conditional(s32[]{:T(128)} %bitcast.30, f32[16,32,1024]{2,1,0:T(8,128)S(1)} %get-tuple-element.183, (s32[]{:T(128)}, f32[16,32,1024]{2,1,0:T(8,128)S(1)}, f32[16,32,1024]{2,1,0:T(8,128)}, f32[1024,1024]{1,0:T(8,128)}) %tuple.41), branch_computations={%region_3.3_spmd, %region_4.4_spmd} | conditional | flops 402685952 | bytes 4588078 | solution.py:42
  214.8 6.1 %fusion.1 = f32[16,32,1024]{2,1,0:T(8,128)S(1)} fusion(f32[16,32,1024]{2,1,0:T(8,128)S(1)} %get-tuple-element.122, s32[]{:T(128)S(6)} %select_n.17, f32[1024,1024]{1,0:T(8,128)} %get-tuple-element.125, f32[16,32,1024]{2,1,0:T(8,128)} %get-tuple-element.124, s32[]{:T(128)} %get-tuple-element.123), kind=kOutput, calls=%fused_computation.2 | convolution fusion | flops 402685952 | bytes 4588036 | tf_op jit(solution)/shard_map/while/body/eval_jaxpr/cond/branch_1_fun/dot_general | solution.py:8
  220.9 0.6 dynamic_slice.34
  222.1 65.8 %all_to_all.18 = f32[16,32,1024]{2,1,0:T(8,128)S(1)} all-to-all(f32[16,32,1024]{2,1,0:T(8,128)S(1)} %get-tuple-element.133), channel_id=1, replica_groups=mesh['node'=16,'dev'=32] {'node'}, dimensions={0} | all-to-all | bytes 4194304 | tf_op jit(solution)/shard_map/all_to_all | solution.py:47
  287.8 1.4 copy.12
  289.3 0.0 copy-start
  289.3 0.0 all-reduce.3.cloned.1.call-update
  290.0 0.1 copy-done
  290.1 0.1 sub.24
  290.2 1.3 dynamic-slice
  291.5 167.0 %all-reduce.3.cloned.1.call-done = f32[1,32,16384]{2,1,0:T(8,128)} async-done(((f32[1,32,16384]{2,1,0:T(8,128)}), f32[1,32,16384]{2,1,0:T(8,128)}) %all-reduce.3.cloned.1.call-update) | async-done | bytes 2097168
  458.5 2.4 dynamic-slice_divide_fusion
  (8 shorter events, 0.1 us)
Async XLA Ops:
  6.5 93.9 %all-gather.4.cloned.1.call-start = ((), (), s32[]{:S(2)}) async-start(), calls=%async_computation.1 | async-start | bytes 4325376 | tf_op jit(solution)/shard_map/all_gather | solution.py:26
  7.3 140.5 %all-gather.6.cloned.1.call-start = ((), (), s32[]{:S(2)}) async-start(), calls=%async_computation.2 | async-start | bytes 2228224 | tf_op jit(solution)/shard_map/all_gather | solution.py:32
  8.0 95.9 %copy-start.1 = (s32[16,256,2]{1,2,0:T(2,128)S(1)}, s32[16,256,2]{1,2,0:T(2,128)}, u32[]{:S(2)}) copy-start(s32[16,256,2]{1,2,0:T(2,128)} %param.13) | copy-start | bytes 98308
  103.9 354.7 %all-reduce.3.cloned.1.call-start = ((), (), s32[]{:S(2)}) async-start(), calls=%async_computation.3 | async-start | bytes 4194304
  289.3 0.8 copy-start
Sparse Core Ops, SparseCore 0:
  10.5 89.9 all-gather.3
  104.0 43.7 all-gather.5
  289.4 169.0 all-reduce.2
where the time goes:
time: 473 us; the launch traced here: 467 us
  waiting for transfers between devices  304 us (64%)
  blocking collectives  65.8 us (14%)
  matrix products  54.9 us (12%)
  between operations  13.8 us (3%)
  local copies, waits for them, and re-layouts  12.5 us (3%)
  loops' own time  9.78 us (2%)
  other arithmetic  6.79 us (1%)
    unnamed x4, waiting for transfers between devices  168 us
    all_gather x1, waiting for transfers between devices, on_device(): lax.all_gather(amps, 'dev', axis=1, tiled=True)[0]  92.5 us
    all_to_all x1, blocking collectives, on_device(): lax.all_to_all(partial_ladder, 'node', split_axis=0, concat_axis=2, tiled...  65.8 us
    dot_general x9, matrix products, tile_product(): lax.dot_general(left, right, (((1,), (1,)), ((), ())), precision=lax.Prec...  54.9 us
    all_gather x1, waiting for transfers between devices, on_device(): piece = lax.all_gather(my_amp[None], 'node', axis=0, tiled=True)  43.5 us
    another operation x1, loops' own time, on_device(): lax.fori_loop(0, piece.shape[0], one_block, jnp.zeros((block_count, pairs...  9.47 us
  transfers between devices with their start and end apart: 3, of which 3 were waited for; matrix products, arithmetic and copies ran while one was open for 1% of the time, Pallas kernels for 0%

commit v1 on v0

v1 whole, which is shorter than its diff:
```python
import functools

import jax
import jax.numpy as jnp
from jax import lax
from jax.experimental import pallas as pl
from jax.experimental.pallas import tpu as pltpu
from jax.sharding import PartitionSpec as P

MESH = pl.DeviceIdType.MESH
NODES = 16
DEVS = 32
NX = 4
NY = 8
NZ = 8
PAIRS = 32
WIDTH = 1024
CHUNKS = ((0, 1), (7, 2), (6, 3), (5, 4))


def kernel(
    amps,
    slots,
    ints,
    tasks,
    out,
    x1,
    x2,
    inv,
    tiles,
    bf,
    bhi,
    blo,
    ahi,
    alo,
    part,
    from_left,
    from_right,
    r1,
    ry,
    r2,
    rz,
    v,
    local_sem,
    send_a,
    recv_a,
    send_c,
    recv_c,
    send_z,
    recv_up,
    recv_down,
    send_sib,
    recv_sib,
    send_x,
    recv_left,
    recv_right,
    send_y,
    recv_y,
    send_n,
    recv_n,
    send_f,
    recv_f,
):
    node = lax.axis_index("node")
    dev = lax.axis_index("dev")
    z, core = node // 2, node % 2
    y, x = dev // NX, dev % NX
    z_up = ((z + 1) % NZ) * 2 + core
    z_down = ((z + NZ - 1) % NZ) * 2 + core
    sibling = z * 2 + 1 - core
    x_right, x_left, x_far = (x + 1) % NX, (x + NX - 1) % NX, (x + 2) % NX

    def remote(src, dst, send, recv, node_id, dev_id):
        return pltpu.make_async_remote_copy(
            src_ref=src,
            dst_ref=dst,
            send_sem=send,
            recv_sem=recv,
            device_id=(node_id, dev_id),
            device_id_type=MESH,
        )

    def drain(ref, sem):
        pltpu.make_async_copy(ref, ref, sem).wait()

    load_b = pltpu.make_async_copy(ints.at[0, 0], bf, local_sem.at[0])
    load_b.start()

    barrier = pltpu.get_barrier_semaphore()

    @pl.loop(1, DEVS)
    def _(k):
        pl.semaphore_signal(barrier, inc=1, device_id=(node, (dev + k) % DEVS), device_id_type=MESH)

    @pl.loop(1, NODES)
    def _(k):
        pl.semaphore_signal(barrier, inc=1, device_id=((node + k) % NODES, dev), device_id_type=MESH)

    pl.semaphore_wait(barrier, DEVS + NODES - 2)

    def tile_of(ref, j):
        rows = pl.ds(pl.multiple_of((j // 8) * 8, 8), 8)
        columns = pl.ds(pl.multiple_of((j % 8) * 128, 128), 128)
        return ref.at[rows, columns]

    own_a = pltpu.make_async_copy(tile_of(amps.at[0, 0], dev), x1.at[dev], local_sem.at[1])
    own_a.start()

    @pl.loop(1, DEVS)
    def _(k):
        j = (dev + k) % DEVS
        remote(tile_of(amps.at[0, 0], j), x1.at[dev], send_a, recv_a, node, j).start()

    @pl.loop(0, DEVS)
    def _(c):
        found = jnp.int32(0)
        for s in range(DEVS):
            found = jnp.where(slots[node, s] == c, jnp.int32(s), found)
        inv[c] = found

    own_a.wait()
    drain(x1.at[pl.ds(0, DEVS - 1)], recv_a)

    own_tile = tiles.at[0, core]

    @pl.loop(1, DEVS)
    def _(k):
        c = (dev + k) % DEVS
        x2[c] = x1[inv[c]]
        remote(x2.at[c], tile_of(own_tile, dev), send_c, recv_c, node, c).start()

    x2[dev] = x1[inv[dev]]
    own_c = pltpu.make_async_copy(x2.at[dev], tile_of(own_tile, dev), local_sem.at[1])
    own_c.start()

    load_b.wait()

    @pl.loop(0, 16)
    def _(i):
        rows = pl.ds(pl.multiple_of(i * 64, 64), 64)
        whole = bf[rows, :]
        high = whole.astype(jnp.bfloat16)
        bhi[rows, :] = high
        blo[rows, :] = (whole - high.astype(jnp.float32)).astype(jnp.bfloat16)

    own_c.wait()
    drain(x1.at[pl.ds(0, DEVS - 1)], recv_c)

    def z_step(step):
        up, down = (NZ - step + 1) % NZ, step - 1
        rows_up = pl.ds(0, 16 if step == 4 else 32)
        rows_down = pl.ds(16, 16) if step == 4 else pl.ds(0, 32)
        remote(
            tiles.at[up, core, rows_up],
            tiles.at[NZ - step, core, rows_up],
            send_z,
            recv_up.at[step - 1],
            z_up,
            dev,
        ).start()
        remote(
            tiles.at[down, core, rows_down],
            tiles.at[step, core, rows_down],
            send_z,
            recv_down.at[step - 1],
            z_down,
            dev,
        ).start()

    def z_wait(step):
        rows_up = pl.ds(0, 16 if step == 4 else 32)
        rows_down = pl.ds(16, 16) if step == 4 else pl.ds(0, 32)
        drain(tiles.at[NZ - step, core, rows_up], recv_up.at[step - 1])
        drain(tiles.at[step, core, rows_down], recv_down.at[step - 1])

    def to_sibling(rel):
        remote(tiles.at[rel, core], tiles.at[rel, core], send_sib, recv_sib.at[rel], sibling, dev).start()

    def compute(q):
        for h, rel in enumerate(CHUNKS[q]):
            drain(tiles.at[rel, 1 - core], recv_sib.at[rel])
            for k in range(2):
                block = ((z + rel) % NZ) * 2 + k
                listed = tasks[block]
                hit = (listed[0:1, :] == node) & (listed[1:2, :] == dev)
                mask = jnp.max(hit.astype(jnp.float32), axis=1, keepdims=True)
                whole = tiles[rel, k] * mask
                high = whole.astype(jnp.bfloat16)
                rows = pl.ds((2 * h + k) * PAIRS, PAIRS)
                ahi[rows, :] = high
                alo[rows, :] = (whole - high.astype(jnp.float32)).astype(jnp.bfloat16)

        @pl.loop(0, 4)
        def _(i):
            columns = pl.ds(pl.multiple_of(i * 256, 256), 256)
            dims = (((1,), (1,)), ((), ()))
            dot = functools.partial(lax.dot_general, dimension_numbers=dims, preferred_element_type=jnp.float32)
            total = dot(ahi[...], blo[columns, :])
            total = total + dot(alo[...], bhi[columns, :])
            total = total + dot(ahi[...], bhi[columns, :])
            for h in range(2):
                for k in range(2):
                    for g in range(4):
                        start = (2 * h + k) * PAIRS + g * 8
                        part[q, g, h, k, :, columns] = total[start : start + 8, :]

    def send_dev(src, dst, recv, x_to):
        send = send_x.at[0 if x_to is x_right else 1]
        remote(src, dst, send, recv, node, y * NX + x_to).start()

    def x_first(q):
        send_dev(part.at[q, x_far, 0], from_left.at[q, 0], recv_left.at[q, 0], x_right)
        send_dev(part.at[q, x_far, 1], from_right.at[q, 0], recv_right.at[q, 0], x_left)
        send_dev(part.at[q, x_right, 1], from_left.at[q, 1], recv_left.at[q, 1], x_right)
        send_dev(part.at[q, x_left, 0], from_right.at[q, 1], recv_right.at[q, 1], x_left)

    def x_second(q):
        drain(from_left.at[q, 0], recv_left.at[q, 0])
        from_left[q, 0] = from_left[q, 0] + part[q, x_right, 0]
        send_dev(from_left.at[q, 0], from_left.at[q, 2], recv_left.at[q, 2], x_right)
        drain(from_right.at[q, 0], recv_right.at[q, 0])
        from_right[q, 0] = from_right[q, 0] + part[q, x_left, 1]
        send_dev(from_right.at[q, 0], from_right.at[q, 2], recv_right.at[q, 2], x_left)

    def x_last(q):
        for ref, sem in ((from_left, recv_left), (from_right, recv_right)):
            for i in (1, 2):
                drain(ref.at[q, i], sem.at[q, i])
        for h in range(2):
            total = part[q, x, h] + from_left[q, 2 - h] + from_right[q, 1 + h]
            for c in range(NY):
                r1[q, c, h] = total[:, :, c * 128 : (c + 1) * 128]
        ry[q, y] = r1[q, y]

        @pl.loop(1, NY)
        def _(k):
            to = (y + k) % NY
            remote(r1.at[q, to], ry.at[q, y], send_y, recv_y.at[q], node, to * NX + x).start()

    def y_last(q):
        drain(ry.at[q, pl.ds(0, NY - 1)], recv_y.at[q])
        total = ry[q, 0]
        for c in range(1, NY):
            total = total + ry[q, c]
        r2[q] = total
        for h, rel in enumerate(CHUNKS[q]):
            for k in range(2):
                to = ((z + rel) % NZ) * 2 + k
                if rel == 0:

                    @pl.when(to == node)
                    def _():
                        rz[node] = r2[q, h, k]

                    @pl.when(to != node)
                    def _():
                        remote(r2.at[q, h, k], rz.at[node], send_n, recv_n, to, dev).start()

                else:
                    remote(r2.at[q, h, k], rz.at[node], send_n, recv_n, to, dev).start()

    z_step(1)
    to_sibling(0)
    z_wait(1)
    z_step(2)
    to_sibling(1)
    to_sibling(7)
    compute(0)
    x_first(0)
    z_wait(2)
    z_step(3)
    to_sibling(2)
    to_sibling(6)
    compute(1)
    x_first(1)
    x_second(0)
    z_wait(3)
    z_step(4)
    to_sibling(3)
    to_sibling(5)
    compute(2)
    x_first(2)
    x_second(1)
    x_last(0)
    z_wait(4)
    to_sibling(4)
    compute(3)
    x_first(3)
    x_second(2)
    x_last(1)
    y_last(0)
    x_second(3)
    x_last(2)
    y_last(1)
    x_last(3)
    y_last(2)
    y_last(3)

    drain(rz.at[pl.ds(0, NODES - 1)], recv_n)
    mine = (y // 2) == x
    columns = pl.ds(pl.multiple_of(y * 128, 128), 128)
    for r in range(8):
        to = 8 * x + r
        v[r] = rz[:, r, :]

        @pl.when(to == dev)
        def _():
            out[:, columns] = rz[:, r, :]

        @pl.when(to != dev)
        def _():
            remote(v.at[r], out.at[:, columns], send_f, recv_f, node, to).start()

    @pl.when(mine)
    def _():
        drain(v.at[pl.ds(0, 7)], recv_f)
        drain(v.at[pl.ds(0, 7)], send_f)

    @pl.when(jnp.logical_not(mine))
    def _():
        drain(v, recv_f)
        drain(v, send_f)

    drain(x1.at[pl.ds(0, DEVS - 1)], send_a)
    drain(x2.at[pl.ds(0, DEVS - 1)], send_c)
    drain(tiles.at[pl.ds(0, 7), 0], send_z)
    drain(tiles.at[:, 0], send_sib)
    drain(from_left, send_x.at[0])
    drain(from_right, send_x.at[1])
    drain(r1.at[:, pl.ds(0, NY - 1)], send_y)
    drain(rz.at[pl.ds(0, NODES - 1)], send_n)


def exchange(amps, slots, ints, tasks):
    f32, bf16 = jnp.float32, jnp.bfloat16
    dma = pltpu.SemaphoreType.DMA
    hbm = pl.BlockSpec(memory_space=pl.ANY)
    vmem = pl.BlockSpec(memory_space=pltpu.VMEM)
    smem = pl.BlockSpec(memory_space=pltpu.SMEM)
    return pl.pallas_call(
        kernel,
        out_shape=jax.ShapeDtypeStruct((NODES, WIDTH), f32),
        in_specs=[hbm, smem, hbm, vmem],
        out_specs=vmem,
        scratch_shapes=[
            pltpu.VMEM((DEVS, 8, 128), f32),
            pltpu.VMEM((DEVS, 8, 128), f32),
            pltpu.SMEM((DEVS,), jnp.int32),
            pltpu.VMEM((NZ, 2, PAIRS, WIDTH), f32),
            pltpu.VMEM((WIDTH, WIDTH), f32),
            pltpu.VMEM((WIDTH, WIDTH), bf16),
            pltpu.VMEM((WIDTH, WIDTH), bf16),
            pltpu.VMEM((4 * PAIRS, WIDTH), bf16),
            pltpu.VMEM((4 * PAIRS, WIDTH), bf16),
            pltpu.VMEM((4, NX, 2, 2, 8, WIDTH), f32),
            pltpu.VMEM((4, 3, 2, 8, WIDTH), f32),
            pltpu.VMEM((4, 3, 2, 8, WIDTH), f32),
            pltpu.VMEM((4, NY, 2, 2, 8, 128), f32),
            pltpu.VMEM((4, NY, 2, 2, 8, 128), f32),
            pltpu.VMEM((4, 2, 2, 8, 128), f32),
            pltpu.VMEM((NODES, 8, 128), f32),
            pltpu.VMEM((8, NODES, 128), f32),
            dma((2,)),
            dma,
            dma,
            dma,
            dma,
            dma,
            dma((4,)),
            dma((4,)),
            dma,
            dma((NZ,)),
            dma((2,)),
            dma((4, 3)),
            dma((4, 3)),
            dma,
            dma((4,)),
            dma,
            dma,
            dma,
            dma,
        ],
        compiler_params=pltpu.CompilerParams(
            collective_id=0, has_side_effects=True, vmem_limit_bytes=48 * 1024 * 1024
        ),
    )(amps, slots, ints, tasks)


def on_device(amps, amp_tile, ints, tasks, pair_energy, virt_energy):
    ladder = exchange(amps, amp_tile, ints, jnp.transpose(tasks, (0, 2, 1)))
    return (ladder / (pair_energy[0, 0] - virt_energy)).reshape(1, 1, -1)


def solution(mesh):
    in_specs = (
        P("node", "dev", None, None),
        P(),
        P("node", "dev", None, None),
        P(),
        P("node", "dev"),
        P(),
    )
    return jax.shard_map(
        on_device, mesh=mesh, in_specs=in_specs, out_specs=P("node", "dev", None), check_vma=False
    )
```

time: 473 us -> 87.4 us (0.18); the launches traced: 467 us -> 86.6 us
  waiting for transfers between devices: 304 us -> 0 us
  Pallas kernels: 0 us -> 80.6 us
  blocking collectives: 65.8 us -> 0 us
  matrix products: 54.9 us -> 0 us
  between operations: 13.8 us -> 0.69 us
  loops' own time: 9.78 us -> 0 us
  local copies, waits for them, and re-layouts: 12.5 us -> 5.25 us
  other arithmetic: 6.79 us -> 0.02 us
    unnamed x4 -> x0, waiting for transfers between devices: 168 us -> none
    all_gather x2 -> x0, waiting for transfers between devices: 136 us -> none  [the longest x1 92.5 us: on_device(): lax.all_gather(amps, 'dev', axis=1, tiled=True)[0]]
    pallas_call x0 -> x1, Pallas kernels: none -> 80.6 us  [exchange(): pl.pallas_call(kernel, out_shape=jax.ShapeDtypeStruct((NODES, WIDTH), f32...]
    all_to_all x1 -> x0, blocking collectives: 65.8 us -> none  [on_device(): lax.all_to_all(partial_ladder, 'node', split_axis=0, concat_axis=2, tiled...]
    dot_general x9 -> x0, matrix products: 54.9 us -> none  [tile_product(): lax.dot_general(left, right, (((1,), (1,)), ((), ())), precision=lax.Prec...]
    another operation x17 -> x0, loops' own time: 9.78 us -> none  [the longest x1 9.47 us: on_device(): lax.fori_loop(0, piece.shape[0], one_block, jnp.zeros((block_count, pairs...]
    dynamic_slice x16 -> x0, local copies, waits for them, and re-layouts: 9.31 us -> none  [one_block(): return lax.cond(hits[position] > 0, add_term, lambda inner: inner, acc)]
  transfers between devices with their start and end apart: 3 -> 0, of which waited for: 3 -> 0; matrix products, arithmetic and copies ran while one was open for 1% -> 0% of each run, Pallas kernels for 0% -> 0%
where the time goes in v1:
time: 87.4 us; the launch traced here: 86.6 us
  Pallas kernels  80.6 us (92%)
  local copies, waits for them, and re-layouts  5.25 us (6%)
    pallas_call x1, Pallas kernels, exchange(): pl.pallas_call(kernel, out_shape=jax.ShapeDtypeStruct((NODES, WIDTH), f32...  80.6 us
    unnamed x10, local copies, waits for them, and re-layouts  4.54 us

profile of v1, /device:TPU:1, one launch (start us, length us, event | category | flops | bytes accessed | tf_op | source)
XLA Modules:
  0.0 86.6 jit_solution(7078533589788930171)
XLA Ops:
  0.7 0.0 copy-start
  0.7 2.2 %copy-done = f32[1,1,1024,1024]{3,2,1,0:T(8,128)S(1)} copy-done((f32[1,1,1024,1024]{3,2,1,0:T(8,128)S(1)}, f32[1,1,1024,1024]{3,2,1,0:T(8,128)}, u32[]{:S(2)}) %copy-start) | copy-done | bytes 4194328
  2.8 0.0 copy-start.1
  2.8 0.9 %copy-done.1 = f32[1,1,32,1024]{3,2,1,0:T(8,128)S(1)} copy-done((f32[1,1,32,1024]{3,2,1,0:T(8,128)S(1)}, f32[1,1,32,1024]{3,2,1,0:T(8,128)}, u32[]{:S(2)}) %copy-start.1) | copy-done | bytes 131096
  3.7 0.0 copy-start.2
  3.7 0.8 copy-done.2
  4.5 0.0 copy-start.3
  4.5 0.7 copy-done.3
  5.2 0.0 copy-start.4
  5.2 80.6 %shard_map.64 = f32[16,1024]{1,0:T(8,128)S(1)} custom-call(f32[1,1,32,1024]{3,2,1,0:T(8,128)S(1)} %copy-done.1, s32[16,32]{1,0:T(8,128)S(1)} %copy-done.3, f32[1,1,1024,1024]{3,2,1,0:T(8,128)S(1)} %copy-done, s32[16,2,256]{2,1,0:T(2,128)S(1)} %bitcast.3), custom_call_target="tpu_custom_call" | custom-call | tf_op jit(solution)/shard_map/pallas_call | solution.py:340
  85.9 0.0 copy-done.4
  85.9 0.7 reshape.3
  (1 shorter events, 0.0 us)
Async XLA Ops:
  0.7 2.2 %copy-start = (f32[1,1,1024,1024]{3,2,1,0:T(8,128)S(1)}, f32[1,1,1024,1024]{3,2,1,0:T(8,128)}, u32[]{:S(2)}) copy-start(f32[1,1,1024,1024]{3,2,1,0:T(8,128)} %ints.1) | copy-start | bytes 12582916
  2.8 0.9 %copy-start.1 = (f32[1,1,32,1024]{3,2,1,0:T(8,128)S(1)}, f32[1,1,32,1024]{3,2,1,0:T(8,128)}, u32[]{:S(2)}) copy-start(f32[1,1,32,1024]{3,2,1,0:T(8,128)} %amps.1) | copy-start | bytes 393220
  3.7 0.8 copy-start.2
  4.5 0.7 copy-start.3
  5.2 80.7 %copy-start.4 = (f32[16,1024]{1,0:T(8,128)S(1)}, f32[16,1024]{1,0:T(8,128)}, u32[]{:S(2)}) copy-start(f32[16,1024]{1,0:T(8,128)} %param.11) | copy-start | bytes 196612

commit v2 on v1

v2 whole, which is shorter than its diff:
```python
import jax
import jax.numpy as jnp
from jax import lax
from jax.experimental import pallas as pl
from jax.experimental.pallas import tpu as pltpu
from jax.sharding import PartitionSpec as P

MESH = pl.DeviceIdType.MESH
NODES = 16
DEVS = 32
NX = 4
NY = 8
NZ = 8
PAIRS = 32
WIDTH = 1024
CHUNKS = ((0,), (7, 1), (6, 2), (5, 3), (4,))
LAST = 4
PIECES = 16


def blocks(q):
    return 2 * len(CHUNKS[q])


def kernel(
    amps,
    slots,
    ints,
    tasks,
    pair_energy,
    virt_energy,
    out,
    x1,
    x2,
    slots_s,
    inv,
    tasks_v,
    energy_s,
    virt_v,
    masks,
    tiles,
    bf,
    bhi,
    blo,
    rows_f,
    rows_b,
    part,
    from_left,
    from_right,
    direct,
    r1,
    ry,
    r2,
    rz,
    sent_x,
    sent_y,
    local_sem,
    send_a,
    recv_a,
    send_c,
    recv_c,
    send_z,
    recv_z,
    send_sib,
    recv_sib,
    send_x,
    recv_left,
    recv_right,
    send_d,
    recv_d,
    send_y,
    recv_y,
    send_n,
    recv_n,
):
    node = lax.axis_index("node")
    dev = lax.axis_index("dev")
    z, core = node // 2, node % 2
    y, x = dev // NX, dev % NX
    sibling = z * 2 + 1 - core
    x_right, x_left, x_far = (x + 1) % NX, (x + NX - 1) % NX, (x + 2) % NX

    def remote(src, dst, send, recv, node_id, dev_id):
        return pltpu.make_async_remote_copy(
            src_ref=src,
            dst_ref=dst,
            send_sem=send,
            recv_sem=recv,
            device_id=(node_id, dev_id),
            device_id_type=MESH,
        )

    def drain(ref, sem):
        pltpu.make_async_copy(ref, ref, sem).wait()

    barrier = pltpu.get_barrier_semaphore()

    @pl.loop(1, DEVS)
    def _(k):
        pl.semaphore_signal(barrier, inc=1, device_id=(node, (dev + k) % DEVS), device_id_type=MESH)

    @pl.loop(1, NODES)
    def _(k):
        pl.semaphore_signal(barrier, inc=1, device_id=((node + k) % NODES, dev), device_id_type=MESH)

    loads = [
        pltpu.make_async_copy(slots, slots_s, local_sem.at[0]),
        pltpu.make_async_copy(tasks, tasks_v, local_sem.at[1]),
        pltpu.make_async_copy(pair_energy, energy_s, local_sem.at[2]),
        pltpu.make_async_copy(virt_energy, virt_v, local_sem.at[3]),
        pltpu.make_async_copy(ints.at[0, 0], bf, local_sem.at[4]),
    ]
    for load in loads:
        load.start()

    pl.semaphore_wait(barrier, DEVS + NODES - 2)

    relay = (dev % 2) == core

    def piece_of(j):
        rows = pl.ds(pl.multiple_of((j % 2) * 16, 16), 16)
        columns = pl.ds(pl.multiple_of((j // 2) * 128, 128), 128)
        return amps.at[0, 0, rows, columns]

    def send_piece(j):
        remote(piece_of(j), x1.at[dev], send_a, recv_a, node, 2 * j + core).start()

    @pl.loop(1, PIECES)
    def _(i):
        send_piece((dev // 2 + i) % PIECES)

    @pl.when(jnp.logical_not(relay))
    def _():
        send_piece(dev // 2)

    own_a = pltpu.make_async_copy(piece_of(dev // 2), x1.at[dev], local_sem.at[5])
    own_c = pltpu.make_async_copy(
        x2.at[dev],
        tiles.at[0, core, dev // 4, pl.ds(pl.multiple_of(((dev // 2) % 2) * 16, 16), 16)],
        local_sem.at[5],
    )

    @pl.when(relay)
    def _():
        own_a.start()

    loads[0].wait()

    @pl.loop(0, DEVS)
    def _(c):
        found = jnp.int32(0)
        for s in range(DEVS):
            found = jnp.where(slots_s[node, s] == c, jnp.int32(s), found)
        inv[c] = found

    @pl.when(relay)
    def _():
        own_a.wait()
        drain(x1.at[pl.ds(0, DEVS - 1)], recv_a)
        own_piece = tiles.at[0, core, dev // 4, pl.ds(pl.multiple_of(((dev // 2) % 2) * 16, 16), 16)]

        @pl.loop(1, DEVS)
        def _(k):
            c = (dev + k) % DEVS
            x2[c] = x1[inv[c]]
            remote(x2.at[c], own_piece, send_c, recv_c, node, c).start()

        x2[dev] = x1[inv[dev]]
        own_c.start()

    loads[4].wait()

    @pl.loop(0, 16)
    def _(i):
        rows = pl.ds(pl.multiple_of(i * 64, 64), 64)
        whole = bf[rows, :]
        high = whole.astype(jnp.bfloat16)
        bhi[rows, :] = high
        blo[rows, :] = (whole - high.astype(jnp.float32)).astype(jnp.bfloat16)

    loads[1].wait()

    @pl.loop(0, NODES)
    def _(i):
        listed = tasks_v[(2 * z + i) % NODES]
        hit = (listed[0:1, :] == node) & (listed[1:2, :] == dev)
        mask = jnp.max(hit.astype(jnp.float32), axis=1, keepdims=True)
        masks[i] = jnp.broadcast_to(mask, (1, 128))

    @pl.when(relay)
    def _():
        own_c.wait()
        drain(x1.at[pl.ds(0, PIECES - 1)], recv_c)

    @pl.when(jnp.logical_not(relay))
    def _():
        drain(x1.at[pl.ds(0, PIECES)], recv_c)

    def z_copy(src, dst, cut, sem, places):
        columns = pl.ds(4 * cut, 4) if cut is not None else pl.ds(0, 8)
        to = ((z + places) % NZ) * 2 + core
        return remote(tiles.at[src, core, columns], tiles.at[dst, core, columns], send_z, sem, to, dev)

    def z_start():
        z_copy(0, 7, None, recv_z.at[0], 1).start()
        z_copy(0, 1, None, recv_z.at[1], NZ - 1).start()
        for h in range(2):
            z_copy(0, 6, h, recv_z.at[2 + h], 2).start()
            z_copy(0, 2, 1 - h, recv_z.at[5 - h], NZ - 2).start()

    def z_near():
        drain(tiles.at[7, core], recv_z.at[0])
        to_sibling(7)
        drain(tiles.at[1, core], recv_z.at[1])
        to_sibling(1)

    def z_forward():
        for h in range(2):
            drain(tiles.at[6, core, pl.ds(4 * h, 4)], recv_z.at[2 + h])
            z_copy(6, 5, h, recv_z.at[6 + h], 1).start()
            if h == 0:
                z_copy(6, 4, 0, recv_z.at[10], 2).start()
            drain(tiles.at[2, core, pl.ds(4 * (1 - h), 4)], recv_z.at[5 - h])
            z_copy(2, 3, 1 - h, recv_z.at[9 - h], NZ - 1).start()
            if h == 0:
                z_copy(2, 4, 1, recv_z.at[11], NZ - 2).start()
        to_sibling(6)
        to_sibling(2)

    def z_far():
        for h in range(2):
            drain(tiles.at[5, core, pl.ds(4 * h, 4)], recv_z.at[6 + h])
            drain(tiles.at[3, core, pl.ds(4 * h, 4)], recv_z.at[8 + h])
        to_sibling(5)
        to_sibling(3)

    def z_opposite():
        for h in range(2):
            drain(tiles.at[4, core, pl.ds(4 * h, 4)], recv_z.at[10 + h])
        to_sibling(4)

    def to_sibling(rel):
        remote(tiles.at[rel, core], tiles.at[rel, core], send_sib, recv_sib.at[rel], sibling, dev).start()

    def compute(q):
        m = blocks(q)
        count = m * PAIRS
        for h, rel in enumerate(CHUNKS[q]):
            drain(tiles.at[rel, 1 - core], recv_sib.at[rel])
            for k in range(2):
                mask = masks[2 * rel + k]
                for g in range(NX):
                    rows_f[:, pl.ds(g * NY * m + 2 * h + k, NY, stride=m), :] = (
                        tiles[rel, k, :, pl.ds(g, NY, stride=NX), :] * mask
                    )
        for c in range(8):
            whole = rows_f[c, 0:count]
            high = whole.astype(jnp.bfloat16)
            rows_b[0:count, c * 128 : (c + 1) * 128] = high
            rows_b[count : 2 * count, c * 128 : (c + 1) * 128] = (whole - high.astype(jnp.float32)).astype(
                jnp.bfloat16
            )

        @pl.loop(0, 4)
        def _(i):
            columns = pl.ds(pl.multiple_of(i * 256, 256), 256)

            def dot(left, right):
                return lax.dot_general(
                    left, right, (((1,), (1,)), ((), ())), preferred_element_type=jnp.float32
                )

            both = dot(rows_b[0 : 2 * count, :], bhi[columns, :])
            low = dot(rows_b[0:count, :], blo[columns, :])
            total = both[0:count, :] + (both[count:, :] + low)
            for g in range(NX):
                for h in range(2):
                    start = (2 * g + h) * 4 * m
                    part[q, g, h, 0 : 4 * m, columns] = total[start : start + 4 * m, :]

    def send_dev(src, dst, side, recv, x_to):
        remote(src, dst, send_x.at[side], recv, node, y * NX + x_to).start()

    def x_first(q):
        rows = pl.ds(0, 4 * blocks(q))

        def own(g, h):
            return part.at[q, g, h, rows]

        if q == LAST:
            for d in (2, 1, 3):
                to = (x + d) % NX
                remote(
                    part.at[q, to, :, rows], direct.at[d - 1], send_d, recv_d.at[d - 1], node, y * NX + to
                ).start()
            return
        send_dev(own(x_far, 0), from_left.at[q, 0, rows], 0, recv_left.at[q, 0], x_right)
        send_dev(own(x_far, 1), from_right.at[q, 0, rows], 1, recv_right.at[q, 0], x_left)
        send_dev(own(x_right, 1), from_left.at[q, 1, rows], 0, recv_left.at[q, 1], x_right)
        send_dev(own(x_left, 0), from_right.at[q, 1, rows], 1, recv_right.at[q, 1], x_left)

    def x_second(q):
        n = 4 * blocks(q)
        rows = pl.ds(0, n)
        drain(from_left.at[q, 0, rows], recv_left.at[q, 0])
        from_left[q, 0, 0:n] = from_left[q, 0, 0:n] + part[q, x_right, 0, 0:n]
        send_dev(from_left.at[q, 0, rows], from_left.at[q, 2, rows], 0, recv_left.at[q, 2], x_right)
        drain(from_right.at[q, 0, rows], recv_right.at[q, 0])
        from_right[q, 0, 0:n] = from_right[q, 0, 0:n] + part[q, x_left, 1, 0:n]
        send_dev(from_right.at[q, 0, rows], from_right.at[q, 2, rows], 1, recv_right.at[q, 2], x_left)

    def x_last(q):
        m = blocks(q)
        n = 4 * m
        rows = pl.ds(0, n)
        if q == LAST:
            for d in range(3):
                drain(direct.at[d], recv_d.at[d])
        else:
            for ref, sem in ((from_left, recv_left), (from_right, recv_right)):
                for i in (1, 2):
                    drain(ref.at[q, i, rows], sem.at[q, i])
        for h in range(2):
            total = part[q, x, h, 0:n]
            if q == LAST:
                total = (total + direct[0, h]) + (direct[1, h] + direct[2, h])
            else:
                total = total + from_left[q, 2 - h, 0:n] + from_right[q, 1 + h, 0:n]
            r1[q, 4 * h : 4 * h + 4, 0:m] = total.reshape(4, m, 8, 128)
        ry[q, y, 0:m] = r1[q, y, 0:m]

        @pl.loop(1, NY)
        def _(k):
            to = (y + k) % NY
            remote(
                r1.at[q, to, pl.ds(0, m)], ry.at[q, y, pl.ds(0, m)], send_y, recv_y.at[q], node, to * NX + x
            ).start()

    def y_last(q):
        m = blocks(q)
        drain(ry.at[q, pl.ds(0, NY - 1), pl.ds(0, m)], recv_y.at[q])
        total = ry[q, 0, 0:m]
        for c in range(1, NY):
            total = total + ry[q, c, 0:m]
        r2[q, 0:m] = total
        for h, rel in enumerate(CHUNKS[q]):
            for k in range(2):
                to = ((z + rel) % NZ) * 2 + k
                src = r2.at[q, 2 * h + k]
                if rel == 0:

                    @pl.when(to == node)
                    def _():
                        rz[node] = r2[q, 2 * h + k]

                    @pl.when(to != node)
                    def _():
                        remote(src, rz.at[node], send_n, recv_n, to, dev).start()

                else:
                    remote(src, rz.at[node], send_n, recv_n, to, dev).start()

    z_start()
    to_sibling(0)
    compute(0)
    x_first(0)
    z_near()
    z_forward()
    compute(1)
    x_first(1)
    x_second(0)
    compute(2)
    x_first(2)
    x_second(1)
    z_far()
    z_opposite()
    x_last(0)
    compute(3)
    x_first(3)
    x_second(2)
    compute(4)
    x_first(4)
    x_second(3)
    x_last(1)
    y_last(0)
    x_last(2)
    y_last(1)
    x_last(3)
    y_last(2)
    loads[2].wait()
    loads[3].wait()
    virt = virt_v[...].reshape(NODES, 8, 128)
    x_last(4)
    y_last(3)
    y_last(4)

    drain(rz.at[pl.ds(0, NODES - 1)], recv_n)
    out[...] = rz[...] / (energy_s[0, 0] - virt)

    @pl.when(relay)
    def _():
        drain(x1.at[pl.ds(0, PIECES - 1)], send_a)
        drain(x2.at[pl.ds(0, DEVS - 1)], send_c)

    @pl.when(jnp.logical_not(relay))
    def _():
        drain(x1.at[pl.ds(0, PIECES)], send_a)

    drain(tiles.at[pl.ds(0, 7), 0], send_z)
    drain(tiles.at[:, 0], send_sib)
    drain(sent_x, send_x.at[0])
    drain(sent_x, send_x.at[1])
    drain(direct, send_d)
    drain(sent_y, send_y)
    drain(rz.at[pl.ds(0, NODES - 1)], send_n)


def exchange(*args):
    f32, bf16, i32 = jnp.float32, jnp.bfloat16, jnp.int32
    dma = pltpu.SemaphoreType.DMA
    return pl.pallas_call(
        kernel,
        out_shape=jax.ShapeDtypeStruct((NODES, 8, 128), f32),
        in_specs=[pl.BlockSpec(memory_space=pltpu.HBM)] * 6,
        out_specs=pl.BlockSpec(memory_space=pltpu.VMEM),
        scratch_shapes=[
            pltpu.VMEM((DEVS, 16, 128), f32),
            pltpu.VMEM((DEVS, 16, 128), f32),
            pltpu.SMEM((NODES, DEVS), i32),
            pltpu.SMEM((DEVS,), i32),
            pltpu.VMEM((NODES, 2, 256), i32),
            pltpu.SMEM((1, 1), f32),
            pltpu.VMEM((NODES, WIDTH), f32),
            pltpu.VMEM((NODES, 1, 128), f32),
            pltpu.VMEM((NZ, 2, 8, PAIRS, 128), f32),
            pltpu.VMEM((WIDTH, WIDTH), f32),
            pltpu.VMEM((WIDTH, WIDTH), bf16),
            pltpu.VMEM((WIDTH, WIDTH), bf16),
            pltpu.VMEM((8, 4 * PAIRS, 128), f32),
            pltpu.VMEM((8 * PAIRS, WIDTH), bf16),
            pltpu.VMEM((5, NX, 2, 16, WIDTH), f32),
            pltpu.VMEM((4, 3, 16, WIDTH), f32),
            pltpu.VMEM((4, 3, 16, WIDTH), f32),
            pltpu.VMEM((3, 2, 8, WIDTH), f32),
            pltpu.VMEM((5, NY, 4, 8, 128), f32),
            pltpu.VMEM((5, NY, 4, 8, 128), f32),
            pltpu.VMEM((5, 4, 8, 128), f32),
            pltpu.VMEM((NODES, 8, 128), f32),
            pltpu.VMEM((7, 3, 8, WIDTH), f32),
            pltpu.VMEM((8, NY - 1, 2, 8, 128), f32),
            dma((6,)),
            dma,
            dma,
            dma,
            dma,
            dma,
            dma((12,)),
            dma,
            dma((NZ,)),
            dma((2,)),
            dma((4, 3)),
            dma((4, 3)),
            dma,
            dma((3,)),
            dma,
            dma((5,)),
            dma,
            dma,
        ],
        compiler_params=pltpu.CompilerParams(
            collective_id=0, has_side_effects=True, vmem_limit_bytes=56 * 1024 * 1024
        ),
    )(*args)


def on_device(amps, amp_tile, ints, tasks, pair_energy, virt_energy):
    tasks = jnp.transpose(tasks, (0, 2, 1))
    return exchange(amps, amp_tile, ints, tasks, pair_energy, virt_energy).reshape(1, 1, -1)


def solution(mesh):
    in_specs = (
        P("node", "dev", None, None),
        P(),
        P("node", "dev", None, None),
        P(),
        P("node", "dev"),
        P(),
    )
    return jax.shard_map(
        on_device, mesh=mesh, in_specs=in_specs, out_specs=P("node", "dev", None), check_vma=False
    )
```

time: 87.4 us -> 80.7 us (0.923)
  local copies, waits for them, and re-layouts: 5.25 us -> 1.47 us
  Pallas kernels: 80.6 us -> 78.1 us
    unnamed x10 -> x1, local copies, waits for them, and re-layouts: 4.54 us -> 1.47 us
    pallas_call x1, Pallas kernels: 80.6 us -> 78.1 us  [exchange(): pl.pallas_call(kernel, out_shape=jax.ShapeDtypeStruct((NODES, 8, 128), f3...]
where the time goes in v2:
time: 80.7 us; the launch traced here: 80.2 us
  Pallas kernels  78.1 us (97%)
  local copies, waits for them, and re-layouts  1.47 us (2%)
    pallas_call x1, Pallas kernels, exchange(): pl.pallas_call(kernel, out_shape=jax.ShapeDtypeStruct((NODES, 8, 128), f3...  78.1 us

profile of v2, /device:TPU:1, one launch (start us, length us, event | category | flops | bytes accessed | tf_op | source)
XLA Modules:
  0.0 80.2 jit_solution(11715469179961924172)
XLA Ops:
  0.7 78.1 %shard_map.64 = f32[16,8,128]{2,1,0:T(8,128)} custom-call(f32[1,1,32,1024]{3,2,1,0:T(8,128)} %amps.1, s32[16,32]{1,0:T(8,128)} %slots.1, f32[1,1,1024,1024]{3,2,1,0:T(8,128)} %ints.1, s32[16,2,256]{2,1,0:T(2,128)} %bitcast.3, f32[1,1]{1,0:T(1,128)S(6)} %copy.8.pair_energy, f32[16,1024]{1,0:T(8,128)} %virt_energy.1), custom_call_target="tpu_custom_call" | custom-call | tf_op jit(solution)/shard_map/pallas_call | solution.py:421
  78.7 1.5 %copy.9 = f32[1,1,16384]{2,1,0:T(1,128)} copy(f32[1,1,16384]{2,1,0:T(1,128)} %bitcast.2) | data formatting | bytes 131072

commit v3 on v2

--- a/solution.py
+++ b/solution.py
@@ -14,7 +14,7 @@
 PAIRS = 32
 WIDTH = 1024
 CHUNKS = ((0,), (7, 1), (6, 2), (5, 3), (4,))
-LAST = 4
+DIRECT = (3, 4)
 PIECES = 16
 
 
@@ -53,6 +53,7 @@
     r2,
     rz,
     sent_x,
+    sent_d,
     sent_y,
     local_sem,
     send_a,
@@ -99,9 +100,9 @@
     def _(k):
         pl.semaphore_signal(barrier, inc=1, device_id=(node, (dev + k) % DEVS), device_id_type=MESH)
 
-    @pl.loop(1, NODES)
-    def _(k):
-        pl.semaphore_signal(barrier, inc=1, device_id=((node + k) % NODES, dev), device_id_type=MESH)
+    pl.semaphore_signal(barrier, inc=1, device_id=(sibling, dev), device_id_type=MESH)
+    for d in (1, NZ - 1):
+        pl.semaphore_signal(barrier, inc=1, device_id=(((z + d) % NZ) * 2 + core, dev), device_id_type=MESH)
 
     loads = [
         pltpu.make_async_copy(slots, slots_s, local_sem.at[0]),
@@ -113,7 +114,7 @@
     for load in loads:
         load.start()
 
-    pl.semaphore_wait(barrier, DEVS + NODES - 2)
+    pl.semaphore_wait(barrier, DEVS + 2)
 
     relay = (dev % 2) == core
 
@@ -196,48 +197,29 @@
     def _():
         drain(x1.at[pl.ds(0, PIECES)], recv_c)
 
-    def z_copy(src, dst, cut, sem, places):
-        columns = pl.ds(4 * cut, 4) if cut is not None else pl.ds(0, 8)
+    def z_copy(src, dst, half, sem, places):
+        columns = pl.ds(4 * half, 4) if half is not None else pl.ds(0, 8)
         to = ((z + places) % NZ) * 2 + core
         return remote(tiles.at[src, core, columns], tiles.at[dst, core, columns], send_z, sem, to, dev)
 
-    def z_start():
-        z_copy(0, 7, None, recv_z.at[0], 1).start()
-        z_copy(0, 1, None, recv_z.at[1], NZ - 1).start()
-        for h in range(2):
-            z_copy(0, 6, h, recv_z.at[2 + h], 2).start()
-            z_copy(0, 2, 1 - h, recv_z.at[5 - h], NZ - 2).start()
-
-    def z_near():
-        drain(tiles.at[7, core], recv_z.at[0])
-        to_sibling(7)
-        drain(tiles.at[1, core], recv_z.at[1])
-        to_sibling(1)
-
-    def z_forward():
-        for h in range(2):
-            drain(tiles.at[6, core, pl.ds(4 * h, 4)], recv_z.at[2 + h])
-            z_copy(6, 5, h, recv_z.at[6 + h], 1).start()
-            if h == 0:
-                z_copy(6, 4, 0, recv_z.at[10], 2).start()
-            drain(tiles.at[2, core, pl.ds(4 * (1 - h), 4)], recv_z.at[5 - h])
-            z_copy(2, 3, 1 - h, recv_z.at[9 - h], NZ - 1).start()
-            if h == 0:
-                z_copy(2, 4, 1, recv_z.at[11], NZ - 2).start()
-        to_sibling(6)
-        to_sibling(2)
-
-    def z_far():
-        for h in range(2):
-            drain(tiles.at[5, core, pl.ds(4 * h, 4)], recv_z.at[6 + h])
-            drain(tiles.at[3, core, pl.ds(4 * h, 4)], recv_z.at[8 + h])
-        to_sibling(5)
-        to_sibling(3)
-
-    def z_opposite():
-        for h in range(2):
-            drain(tiles.at[4, core, pl.ds(4 * h, 4)], recv_z.at[10 + h])
-        to_sibling(4)
+    def z_send_up(step):
+        z_copy((NZ - step + 1) % NZ, NZ - step, 0 if step == 4 else None, recv_z.at[2 * step - 2], 1).start()
+
+    def z_send_down(step):
+        z_copy(step - 1, step, 1 if step == 4 else None, recv_z.at[2 * step - 1], NZ - 1).start()
+
+    def z_advance(step):
+        if step == 4:
+            for h in range(2):
+                drain(tiles.at[4, core, pl.ds(4 * h, 4)], recv_z.at[6 + h])
+            to_sibling(4)
+            return
+        drain(tiles.at[NZ - step, core], recv_z.at[2 * step - 2])
+        z_send_up(step + 1)
+        to_sibling(NZ - step)
+        drain(tiles.at[step, core], recv_z.at[2 * step - 1])
+        z_send_down(step + 1)
+        to_sibling(step)
 
     def to_sibling(rel):
         remote(tiles.at[rel, core], tiles.at[rel, core], send_sib, recv_sib.at[rel], sibling, dev).start()
@@ -287,11 +269,17 @@
         def own(g, h):
             return part.at[q, g, h, rows]
 
-        if q == LAST:
+        if q in DIRECT:
+            i = DIRECT.index(q)
             for d in (2, 1, 3):
                 to = (x + d) % NX
                 remote(
-                    part.at[q, to, :, rows], direct.at[d - 1], send_d, recv_d.at[d - 1], node, y * NX + to
+                    part.at[q, to, :, rows],
+                    direct.at[i, d - 1, :, rows],
+                    send_d,
+                    recv_d.at[i, d - 1],
+                    node,
+                    y * NX + to,
                 ).start()
             return
         send_dev(own(x_far, 0), from_left.at[q, 0, rows], 0, recv_left.at[q, 0], x_right)
@@ -313,17 +301,18 @@
         m = blocks(q)
         n = 4 * m
         rows = pl.ds(0, n)
-        if q == LAST:
+        if q in DIRECT:
+            i = DIRECT.index(q)
             for d in range(3):
-                drain(direct.at[d], recv_d.at[d])
+                drain(direct.at[i, d, :, rows], recv_d.at[i, d])
         else:
             for ref, sem in ((from_left, recv_left), (from_right, recv_right)):
                 for i in (1, 2):
                     drain(ref.at[q, i, rows], sem.at[q, i])
         for h in range(2):
             total = part[q, x, h, 0:n]
-            if q == LAST:
-                total = (total + direct[0, h]) + (direct[1, h] + direct[2, h])
+            if q in DIRECT:
+                total = (total + direct[i, 0, h, 0:n]) + (direct[i, 1, h, 0:n] + direct[i, 2, h, 0:n])
             else:
                 total = total + from_left[q, 2 - h, 0:n] + from_right[q, 1 + h, 0:n]
             r1[q, 4 * h : 4 * h + 4, 0:m] = total.reshape(4, m, 8, 128)
@@ -360,29 +349,29 @@
                 else:
                     remote(src, rz.at[node], send_n, recv_n, to, dev).start()
 
-    z_start()
+    z_send_up(1)
+    z_send_down(1)
     to_sibling(0)
     compute(0)
     x_first(0)
-    z_near()
-    z_forward()
+    z_advance(1)
     compute(1)
     x_first(1)
     x_second(0)
+    z_advance(2)
     compute(2)
     x_first(2)
     x_second(1)
-    z_far()
-    z_opposite()
     x_last(0)
+    z_advance(3)
     compute(3)
     x_first(3)
     x_second(2)
+    x_last(1)
+    y_last(0)
+    z_advance(4)
     compute(4)
     x_first(4)
-    x_second(3)
-    x_last(1)
-    y_last(0)
     x_last(2)
     y_last(1)
     x_last(3)
@@ -410,7 +399,7 @@
     drain(tiles.at[:, 0], send_sib)
     drain(sent_x, send_x.at[0])
     drain(sent_x, send_x.at[1])
-    drain(direct, send_d)
+    drain(sent_d, send_d)
     drain(sent_y, send_y)
     drain(rz.at[pl.ds(0, NODES - 1)], send_n)
 
@@ -439,14 +428,15 @@
             pltpu.VMEM((8, 4 * PAIRS, 128), f32),
             pltpu.VMEM((8 * PAIRS, WIDTH), bf16),
             pltpu.VMEM((5, NX, 2, 16, WIDTH), f32),
-            pltpu.VMEM((4, 3, 16, WIDTH), f32),
-            pltpu.VMEM((4, 3, 16, WIDTH), f32),
-            pltpu.VMEM((3, 2, 8, WIDTH), f32),
+            pltpu.VMEM((3, 3, 16, WIDTH), f32),
+            pltpu.VMEM((3, 3, 16, WIDTH), f32),
+            pltpu.VMEM((2, 3, 2, 16, WIDTH), f32),
             pltpu.VMEM((5, NY, 4, 8, 128), f32),
             pltpu.VMEM((5, NY, 4, 8, 128), f32),
             pltpu.VMEM((5, 4, 8, 128), f32),
             pltpu.VMEM((NODES, 8, 128), f32),
-            pltpu.VMEM((7, 3, 8, WIDTH), f32),
+            pltpu.VMEM((5, 3, 8, WIDTH), f32),
+            pltpu.VMEM((3, 6, 8, WIDTH), f32),
             pltpu.VMEM((8, NY - 1, 2, 8, 128), f32),
             dma((6,)),
             dma,
@@ -454,14 +444,14 @@
             dma,
             dma,
             dma,
-            dma((12,)),
+            dma((8,)),
             dma,
             dma((NZ,)),
             dma((2,)),
-            dma((4, 3)),
-            dma((4, 3)),
-            dma,
-            dma((3,)),
+            dma((3, 3)),
+            dma((3, 3)),
+            dma,
+            dma((2, 3)),
             dma,
             dma((5,)),
             dma,

time: 80.7 us -> 77.5 us (0.960)
  Pallas kernels: 78.1 us -> 75.2 us
    pallas_call x1, Pallas kernels: 78.1 us -> 75.2 us  [exchange(): pl.pallas_call(kernel, out_shape=jax.ShapeDtypeStruct((NODES, 8, 128), f3...]
where the time goes in v3:
time: 77.5 us; the launch traced here: 77.3 us
  Pallas kernels  75.2 us (97%)
  local copies, waits for them, and re-layouts  1.47 us (2%)
    pallas_call x1, Pallas kernels, exchange(): pl.pallas_call(kernel, out_shape=jax.ShapeDtypeStruct((NODES, 8, 128), f3...  75.2 us

profile of v3, /device:TPU:1, one launch (start us, length us, event | category | flops | bytes accessed | tf_op | source)
XLA Modules:
  0.0 77.3 jit_solution(12473355279382941314)
XLA Ops:
  0.7 75.2 %shard_map.64 = f32[16,8,128]{2,1,0:T(8,128)} custom-call(f32[1,1,32,1024]{3,2,1,0:T(8,128)} %amps.1, s32[16,32]{1,0:T(8,128)} %slots.1, f32[1,1,1024,1024]{3,2,1,0:T(8,128)} %ints.1, s32[16,2,256]{2,1,0:T(2,128)} %bitcast.3, f32[1,1]{1,0:T(1,128)S(6)} %copy.8.pair_energy, f32[16,1024]{1,0:T(8,128)} %virt_energy.1), custom_call_target="tpu_custom_call" | custom-call | tf_op jit(solution)/shard_map/pallas_call | solution.py:410
  75.9 1.5 %copy.9 = f32[1,1,16384]{2,1,0:T(1,128)} copy(f32[1,1,16384]{2,1,0:T(1,128)} %bitcast.2) | data formatting | bytes 131072
